TPU v7x, 512 devices: a whole 4x4x16 slice. The times are simulated.
512 devices in a mesh: seq: 128 (over x, z, core), head: 4 (over y).
Axes of the slice: x: 4, y: 4, z: 16, core: 2. Of those that a mesh axis runs over, the one named last changes fastest.
Arguments:
- queries: bfloat16 [65536, 2048], P('seq', 'head'), may hold values from -6 to 6
- keys: bfloat16 [65536, 2048], P('seq', 'head'), may hold values from -6 to 6
- values: bfloat16 [65536, 2048], P('seq', 'head'), may hold values from -6 to 6
- summary_lists: int32 [128, 8, 16], P('seq', 'head'), may hold values from 0 to 126, as said below
- out_weight: bfloat16 [2048, 2048], P('head'), may hold values from -0.125 to 0.125
Outputs:
- mixed: bfloat16 [65536, 2048], P(('seq', 'head'))
Inputs may be any that keep to these rules, and one draw needn't show every extreme that they name: `summary_lists`: entry [b, f, k] names a block. In every query block b above 0 it is below b, and entry [b, f, 0] is b - 1; in query block 0 every entry is 0 and names nothing. Entries may repeat.
All inputs are finite; a program needn't handle non-finite values.
Results may differ from a plain program's by a relative error of at most 0.014.
Values may be sent and summed in bfloat16 or wider, within the bound.
A program may use at most 64 MiB of HBM per device.

v0:
```python
import math
import jax
import jax.numpy as jnp
from jax import lax
from jax.sharding import PartitionSpec as P

HEAD_DIM = 128
BLK = 512
SUMMARY = 32
ROWS_DEV = 1
NEG = -1e30


def softmax_rounded(scores, valid):
    scores = jnp.where(valid, scores, NEG)
    peak = jnp.max(scores, axis=-1, keepdims=True)
    weights = jnp.where(valid, jnp.exp(scores - peak), 0.0)
    return (weights / jnp.sum(weights, axis=-1, keepdims=True)).astype(jnp.bfloat16)


def column_attend(pieces):
    col_q, col_k, col_v = pieces
    scale = HEAD_DIM ** (-0.5)
    scores = jnp.einsum("rxcd,sxcd->xcrs", col_q, col_k, preferred_element_type=jnp.float32) * scale
    blocks = col_q.shape[0]
    earlier = jnp.arange(blocks)[:, None] >= jnp.arange(blocks)[None, :]
    weights = softmax_rounded(scores, earlier)
    return jnp.einsum("xcrs,sxcd->rxcd", weights, col_v, preferred_element_type=jnp.float32).astype(
        jnp.bfloat16
    )


def absorb(state, scores, multiplier):
    old_peak, old_denom = (state[0], state[1])
    new_peak = jnp.maximum(old_peak, jnp.max(scores, axis=(3, 4)))
    weights = jnp.exp(scores - new_peak[..., None, None]) * multiplier[:, :, None, :, None]
    shrink = jnp.exp(old_peak - new_peak)
    return (new_peak, old_denom * shrink + jnp.sum(weights, axis=(3, 4)), shrink, weights)


def per_device(queries, keys, values, summary_lists, out_weight):
    scale = HEAD_DIM ** (-0.5)
    seq_count = lax.axis_size("seq")
    query_heads = queries.reshape(ROWS_DEV, BLK, 4, HEAD_DIM)
    key_heads = keys.reshape(ROWS_DEV, BLK, 4, HEAD_DIM)
    value_heads = values.reshape(ROWS_DEV, BLK, 4, HEAD_DIM)
    causal = jnp.arange(BLK)[:, None] >= jnp.arange(BLK)[None, :]
    block_index = lax.axis_index("seq") * ROWS_DEV + jnp.arange(ROWS_DEV, dtype=jnp.int32)

    def column_layout(source):
        return source[:, :, 1].reshape(ROWS_DEV, seq_count, BLK // seq_count, HEAD_DIM)

    column_moved = column_attend(
        (
            lax.all_to_all(
                column_layout(query_heads), "seq", split_axis=1, concat_axis=0, tiled=True
            ),
            lax.all_to_all(
                column_layout(key_heads), "seq", split_axis=1, concat_axis=0, tiled=True
            ),
            lax.all_to_all(
                column_layout(value_heads), "seq", split_axis=1, concat_axis=0, tiled=True
            ),
        )
    )
    row_scores = (
        jnp.einsum(
            "rid,rjd->rij",
            query_heads[:, :, 0],
            key_heads[:, :, 0],
            preferred_element_type=jnp.float32,
        )
        * scale
    )
    row_weights = softmax_rounded(row_scores, causal)
    row_out = jnp.einsum(
        "rij,rjd->rid", row_weights, value_heads[:, :, 0], preferred_element_type=jnp.float32
    ).astype(jnp.bfloat16)
    fixed_q = query_heads[:, :, 2:]
    fixed_k = key_heads[:, :, 2:]
    fixed_v = value_heads[:, :, 2:]
    own_scores = (
        jnp.einsum("rifd,rjfd->rfij", fixed_q, fixed_k, preferred_element_type=jnp.float32) * scale
    )
    own_scores = jnp.where(causal, own_scores, NEG)
    own_peak = jnp.max(own_scores, axis=-1)
    own_weights = jnp.exp(own_scores - own_peak[..., None])
    own_denom = jnp.sum(own_weights, axis=-1)
    own_sum = jnp.einsum(
        "rfij,rjfd->rfid",
        own_weights.astype(jnp.bfloat16),
        fixed_v,
        preferred_element_type=jnp.float32,
    )
    tail_k = jnp.swapaxes(fixed_k[:, BLK - SUMMARY :], 1, 2)
    tail_v = jnp.swapaxes(fixed_v[:, BLK - SUMMARY :], 1, 2)
    piece_k = lax.all_gather(tail_k, "seq", axis=0, tiled=True)
    piece_v = lax.all_gather(tail_v, "seq", axis=0, tiled=True)
    arrived = piece_k.shape[0]
    stride = math.gcd(arrived, 8)

    def inner(turn, running):
        offset = turn * stride
        part_k = lax.dynamic_slice_in_dim(piece_k, offset, stride, 0)
        part_v = lax.dynamic_slice_in_dim(piece_v, offset, stride, 0)
        tile_index = offset + jnp.arange(stride, dtype=jnp.int32)
        matches = (summary_lists[:, :, :, None] == tile_index) & (
            tile_index < block_index[:, None, None, None]
        )
        multiplier = jnp.sum(matches.astype(jnp.float32), axis=2)
        scores = (
            jnp.einsum("rifd,nfcd->rfinc", fixed_q, part_k, preferred_element_type=jnp.float32)
            * scale
        )
        scores = jnp.where(multiplier[:, :, None, :, None] > 0, scores, NEG)
        new_peak, new_denom, shrink, weights = absorb(running, scores, multiplier)
        new_sum = running[2] * shrink[..., None] + jnp.einsum(
            "rfinc,nfcd->rfid",
            weights.astype(jnp.bfloat16),
            part_v,
            preferred_element_type=jnp.float32,
        )
        return (new_peak, new_denom, new_sum)

    final_peak, final_denom, final_sum = lax.fori_loop(
        0, arrived // stride, inner, (own_peak, own_denom, own_sum)
    )
    fixed_out = jnp.swapaxes((final_sum / final_denom[..., None]).astype(jnp.bfloat16), 1, 2)
    column_out = lax.all_to_all(
        column_moved, "seq", split_axis=0, concat_axis=1, tiled=True
    ).reshape(ROWS_DEV, BLK, HEAD_DIM)
    attended = jnp.concatenate(
        [row_out[:, :, None], column_out[:, :, None], fixed_out], axis=2
    ).reshape(ROWS_DEV * BLK, 4 * HEAD_DIM)
    return lax.psum_scatter(
        jnp.dot(attended, out_weight, preferred_element_type=jnp.float32).astype(jnp.bfloat16),
        "head",
        scatter_dimension=0,
        tiled=True,
    )


def solution(mesh):
    return jax.shard_map(
        per_device,
        mesh=mesh,
        in_specs=(
            P("seq", "head"),
            P("seq", "head"),
            P("seq", "head"),
            P("seq", "head", None),
            P("head", None),
        ),
        out_specs=P(("seq", "head"), None),
        check_vma=False,
    )
```

profile of v0, /device:TPU:1, one launch (start us, length us, event | category | flops | bytes accessed | tf_op | source)
XLA Modules:
  0.0 376.9 jit_solution(72792832093655614)
XLA Ops:
  6.5 1.4 copy.55
  8.9 1.3 copy.56
  11.0 1.3 copy.54
  13.0 20.4 %all-to-all-start = ((bf16[1,128,4,128]{3,2,0,1:T(4,128)(2,1)}), bf16[1,128,4,128]{3,2,0,1:T(4,128)(2,1)S(1)}, u32[]{:S(2)}, u32[]{:S(2)}) async-start(bf16[1,128,4,128]{3,2,0,1:T(4,128)(2,1)} %bitcast.23), calls=%async_computation | async-start | bytes 262144 | tf_op jit(solution)/shard_map/all_to_all | solution.py:55
  34.1 1.3 fusion.47
  35.5 15.8 %all-to-all-done = bf16[1,128,4,128]{3,2,0,1:T(4,128)(2,1)S(1)} async-done(((bf16[1,128,4,128]{3,2,0,1:T(4,128)(2,1)}), bf16[1,128,4,128]{3,2,0,1:T(4,128)(2,1)S(1)}, u32[]{:S(2)}, u32[]{:S(2)}) %all-to-all-start) | async-done | bytes 131104 | tf_op jit(solution)/shard_map/all_to_all | solution.py:55
  51.3 6.7 %all-to-all-start.1 = ((bf16[1,128,4,128]{3,2,0,1:T(4,128)(2,1)}), bf16[1,128,4,128]{3,2,0,1:T(4,128)(2,1)S(1)}, u32[]{:S(2)}, u32[]{:S(2)}) async-start(bf16[1,128,4,128]{3,2,0,1:T(4,128)(2,1)} %bitcast.26), calls=%async_computation.1 | async-start | bytes 262144 | tf_op jit(solution)/shard_map/all_to_all | solution.py:58
  59.8 1.4 fusion.30
  61.1 2.9 fusion.15
  64.0 11.7 %all-to-all-done.1 = bf16[1,128,4,128]{3,2,0,1:T(4,128)(2,1)S(1)} async-done(((bf16[1,128,4,128]{3,2,0,1:T(4,128)(2,1)}), bf16[1,128,4,128]{3,2,0,1:T(4,128)(2,1)S(1)}, u32[]{:S(2)}, u32[]{:S(2)}) %all-to-all-start.1) | async-done | bytes 131104 | tf_op jit(solution)/shard_map/all_to_all | solution.py:58
  75.7 6.7 %all-to-all-start.2 = ((bf16[1,128,4,128]{3,2,0,1:T(4,128)(2,1)}), bf16[1,128,4,128]{3,2,0,1:T(4,128)(2,1)S(1)}, u32[]{:S(2)}, u32[]{:S(2)}) async-start(bf16[1,128,4,128]{3,2,0,1:T(4,128)(2,1)} %bitcast.29), calls=%async_computation.2 | async-start | bytes 262144 | tf_op jit(solution)/shard_map/all_to_all | solution.py:61
  83.3 2.3 fusion.23
  85.8 14.3 %all-to-all-done.2 = bf16[1,128,4,128]{3,2,0,1:T(4,128)(2,1)S(1)} async-done(((bf16[1,128,4,128]{3,2,0,1:T(4,128)(2,1)}), bf16[1,128,4,128]{3,2,0,1:T(4,128)(2,1)S(1)}, u32[]{:S(2)}, u32[]{:S(2)}) %all-to-all-start.2) | async-done | bytes 131104 | tf_op jit(solution)/shard_map/all_to_all | solution.py:61
  101.1 6.8 %all-to-all-start.3 = ((bf16[128,1,4,128]{3,2,1,0:T(4,128)(2,1)}), bf16[128,1,4,128]{3,2,1,0:T(4,128)(2,1)S(1)}, u32[]{:S(2)}, u32[]{:S(2)}) async-start(bf16[128,1,4,128]{3,2,1,0:T(4,128)(2,1)} %copy.67), calls=%async_computation.3 | async-start | bytes 262144 | tf_op jit(solution)/shard_map/all_to_all | solution.py:129
  108.2 2.2 fusion.17
  110.4 1.7 convolution_bitcast_fusion.1
  112.1 13.7 %all-to-all-done.3 = bf16[128,1,4,128]{3,2,1,0:T(4,128)(2,1)S(1)} async-done(((bf16[128,1,4,128]{3,2,1,0:T(4,128)(2,1)}), bf16[128,1,4,128]{3,2,1,0:T(4,128)(2,1)S(1)}, u32[]{:S(2)}, u32[]{:S(2)}) %all-to-all-start.3) | async-done | bytes 131104 | tf_op jit(solution)/shard_map/all_to_all | solution.py:129
  125.9 32.0 %all-gather.3.cloned.1.call-done = bf16[128,2,32,128]{3,2,1,0:T(8,128)(2,1)} async-done(((bf16[1,2,32,128]{3,2,1,0:T(8,128)(2,1)}), bf16[128,2,32,128]{3,2,1,0:T(8,128)(2,1)}) %all-gather.3.cloned.1.call-update) | async-done | bytes 2097168 | tf_op jit(solution)/shard_map/all_gather | solution.py:97
  157.9 140.1 %all-gather.5.cloned.1.call-done = bf16[128,2,32,128]{3,2,1,0:T(8,128)(2,1)} async-done(((bf16[1,2,32,128]{3,2,1,0:T(8,128)(2,1)}), bf16[128,2,32,128]{3,2,1,0:T(8,128)(2,1)}) %all-gather.5.cloned.1.call-update) | async-done | bytes 2097168 | tf_op jit(solution)/shard_map/all_gather | solution.py:98
  298.1 36.2 %while.17 = (s32[]{:T(128)}, f32[1,2,512]{2,1,0:T(2,128)S(1)}, f32[1,2,512]{2,1,0:T(2,128)S(1)}, f32[1,2,512,128]{2,3,1,0:T(8,128)S(1)}, s32[1,2,16]{2,1,0:T(2,1...) while((s32[]{:T(128)}, f32[1,2,512]{2,1,0:T(2,128)S(1)}, ...), condition=%wide.region_10.11_spmd, body=%wide.region_6.10_spmd.sunk | while | flops 136843296 | bytes 5309099 | solution.py:125
  298.1 1.0 constant_dynamic-slice_fusion.3
  302.6 1.0 constant_dynamic-slice_fusion.3
  304.9 1.0 constant_dynamic-slice_fusion.3
  307.1 1.0 constant_dynamic-slice_fusion.3
  311.6 1.0 constant_dynamic-slice_fusion.3
  318.4 1.0 constant_dynamic-slice_fusion.3
  320.7 1.0 constant_dynamic-slice_fusion.3
  322.9 1.0 constant_dynamic-slice_fusion.3
  325.2 1.0 constant_dynamic-slice_fusion.3
  329.7 1.0 constant_dynamic-slice_fusion.3
  334.4 2.6 convolution_convert_fusion
  337.0 33.4 %reduce-scatter.2.cloned.1.call-done = bf16[128,2048]{1,0:T(8,128)(2,1)} async-done(((bf16[512,2048]{1,0:T(8,128)(2,1)}), bf16[128,2048]{1,0:T(8,128)(2,1)}) %reduce-scatter.2.cloned.1.call-update) | async-done | bytes 524304 | tf_op jit(solution)/shard_map/reduce_scatter | solution.py:135
  (206 shorter events, 32.7 us)
Async XLA Ops:
  6.5 327.8 %copy-start = (bf16[512,2048]{1,0:T(8,128)(2,1)S(1)}, bf16[512,2048]{1,0:T(8,128)(2,1)}, u32[]{:S(2)}) copy-start(bf16[512,2048]{1,0:T(8,128)(2,1)} %param.11) | copy-start | bytes 6291460
  6.5 151.4 %all-gather.3.cloned.1.call-start = ((), (), s32[]{:S(2)}) async-start(), calls=%async_computation.5 | async-start | bytes 2113536 | tf_op jit(solution)/shard_map/all_gather | solution.py:97
  7.9 27.5 %copy-start.3 = (bf16[512,512]{0,1:T(8,128)(2,1)}, bf16[512,512]{0,1:T(8,128)(2,1)S(1)}, u32[]{:S(2)}) copy-start(bf16[512,512]{0,1:T(8,128)(2,1)S(1)} %copy.55) | copy-start | bytes 1572868
  8.8 289.2 %all-gather.5.cloned.1.call-start = ((), (), s32[]{:S(2)}) async-start(), calls=%async_computation.6 | async-start | bytes 2113536 | tf_op jit(solution)/shard_map/all_gather | solution.py:98
  10.1 0.8 copy-start.2
  13.0 38.3 %all-to-all-start = ((bf16[1,128,4,128]{3,2,0,1:T(4,128)(2,1)}), bf16[1,128,4,128]{3,2,0,1:T(4,128)(2,1)S(1)}, u32[]{:S(2)}, u32[]{:S(2)}) async-start(bf16[1,128,4,128]{3,2,0,1:T(4,128)(2,1)} %bitcast.23), calls=%async_computation | async-start | bytes 262144 | tf_op jit(solution)/shard_map/all_to_all | solution.py:55
  51.3 24.4 %all-to-all-start.1 = ((bf16[1,128,4,128]{3,2,0,1:T(4,128)(2,1)}), bf16[1,128,4,128]{3,2,0,1:T(4,128)(2,1)S(1)}, u32[]{:S(2)}, u32[]{:S(2)}) async-start(bf16[1,128,4,128]{3,2,0,1:T(4,128)(2,1)} %bitcast.26), calls=%async_computation.1 | async-start | bytes 262144 | tf_op jit(solution)/shard_map/all_to_all | solution.py:58
  75.7 24.4 %all-to-all-start.2 = ((bf16[1,128,4,128]{3,2,0,1:T(4,128)(2,1)}), bf16[1,128,4,128]{3,2,0,1:T(4,128)(2,1)S(1)}, u32[]{:S(2)}, u32[]{:S(2)}) async-start(bf16[1,128,4,128]{3,2,0,1:T(4,128)(2,1)} %bitcast.29), calls=%async_computation.2 | async-start | bytes 262144 | tf_op jit(solution)/shard_map/all_to_all | solution.py:61
  83.3 2.3 copy-start.6
  101.1 24.7 %all-to-all-start.3 = ((bf16[128,1,4,128]{3,2,1,0:T(4,128)(2,1)}), bf16[128,1,4,128]{3,2,1,0:T(4,128)(2,1)S(1)}, u32[]{:S(2)}, u32[]{:S(2)}) async-start(bf16[128,1,4,128]{3,2,1,0:T(4,128)(2,1)} %copy.67), calls=%async_computation.3 | async-start | bytes 262144 | tf_op jit(solution)/shard_map/all_to_all | solution.py:129
  107.9 262.5 %reduce-scatter.2.cloned.1.call-start = ((), (), s32[]{:S(2)}) async-start(), calls=%async_computation.7 | async-start | bytes 2621440 | tf_op jit(solution)/shard_map/reduce_scatter | solution.py:135
  108.2 2.2 copy-start.1
  110.4 187.6 %copy-start.5 = (s32[1,2,16]{2,1,0:T(2,128)S(1)}, s32[1,2,16]{2,1,0:T(2,128)}, u32[]{:S(2)}) copy-start(s32[1,2,16]{2,1,0:T(2,128)} %param.10) | copy-start | bytes 388
  298.1 36.2 %copy-start.4 = (bf16[1,512,1,128]{1,3,2,0:T(8,128)(2,1)S(1)}, bf16[1,512,1,128]{1,3,2,0:T(8,128)(2,1)}, u32[]{:S(2)}) copy-start(bf16[1,512,1,128]{1,3,2,0:T(8,128)(2,1)} %fusion.23) | copy-start | bytes 393220
Sparse Core Ops, SparseCore 0:
  10.5 147.4 all-gather.2
  161.1 136.9 all-gather.4
  337.1 33.2 reduce-scatter.1
where the time goes:
time: 378 us; the launch traced here: 377 us
  waiting for transfers between devices  261 us (69%)
  starting transfers between devices  40.9 us (11%)
  local copies, waits for them, and re-layouts  25.7 us (7%)
  matrix products  23.2 us (6%)
  between operations  13.3 us (4%)
  other arithmetic  11.7 us (3%)
    all_gather x1, waiting for transfers between devices, per_device(): piece_v = lax.all_gather(tail_v, 'seq', axis=0, tiled=True)  140 us
    reduce_scatter x1, waiting for transfers between devices, per_device(): lax.psum_scatter(jnp.dot(attended, out_weight, preferred_element_type=jnp...  33.4 us
    all_gather x1, waiting for transfers between devices, per_device(): piece_k = lax.all_gather(tail_k, 'seq', axis=0, tiled=True)  32 us
    all_to_all x1, starting transfers between devices, per_device(): lax.all_to_all(column_layout(query_heads), 'seq', split_axis=1, concat_ax...  20.4 us
    dynamic_slice x16, local copies, waits for them, and re-layouts, inner(): part_v = lax.dynamic_slice_in_dim(piece_v, offset, stride, 0)  15.9 us
    all_to_all x1, waiting for transfers between devices, per_device(): lax.all_to_all(column_layout(query_heads), 'seq', split_axis=1, concat_ax...  15.8 us
    all_to_all x1, waiting for transfers between devices, per_device(): lax.all_to_all(column_layout(value_heads), 'seq', split_axis=1, concat_ax...  14.3 us
    all_to_all x1, waiting for transfers between devices, per_device(): lax.all_to_all(column_moved, 'seq', split_axis=0, concat_axis=1, tiled=True)  13.7 us
  transfers between devices with their start and end apart: 7, of which 7 were waited for; matrix products, arithmetic and copies ran while one was open for 5% of the time, Pallas kernels for 0%

commit v1 on v0

--- a/solution.py
+++ b/solution.py
@@ -9,6 +9,11 @@
 SUMMARY = 32
 ROWS_DEV = 1
 NEG = -1e30
+keep_up_numbers = lambda xs, t0, a_name: jnp.split(
+    jax.lax.all_gather(jnp.concatenate([xs, t0], axis=1), a_name, axis=0, tiled=True),
+    [xs.shape[1]],
+    axis=1,
+)
 
 
 def softmax_rounded(scores, valid):
@@ -94,8 +99,7 @@
     )
     tail_k = jnp.swapaxes(fixed_k[:, BLK - SUMMARY :], 1, 2)
     tail_v = jnp.swapaxes(fixed_v[:, BLK - SUMMARY :], 1, 2)
-    piece_k = lax.all_gather(tail_k, "seq", axis=0, tiled=True)
-    piece_v = lax.all_gather(tail_v, "seq", axis=0, tiled=True)
+    piece_k, piece_v = keep_up_numbers(tail_k, tail_v, "seq")
     arrived = piece_k.shape[0]
     stride = math.gcd(arrived, 8)
 

time: 378 us -> 245 us (0.65)
  waiting for transfers between devices: 261 us -> 123 us
  local copies, waits for them, and re-layouts: 25.7 us -> 29.8 us
    all_gather x2 -> x1, waiting for transfers between devices: 172 us -> 32.5 us  [jax.lax.all_gather(jnp.concatenate([xs, t0], axis=1), a_name, axis=0, til...]
    split x0 -> x1, local copies, waits for them, and re-layouts: none -> 5.18 us  [jnp.split(jax.lax.all_gather(jnp.concatenate([xs, t0], axis=1), a_name, a...]
  transfers between devices with their start and end apart: 7 -> 6, of which waited for: 7 -> 6; matrix products, arithmetic and copies ran while one was open for 5% -> 8% of each run, Pallas kernels for 0% -> 0%
where the time goes in v1:
time: 245 us; the launch traced here: 244 us
  waiting for transfers between devices  123 us (50%)
  starting transfers between devices  40.8 us (17%)
  local copies, waits for them, and re-layouts  29.8 us (12%)
  matrix products  23.2 us (9%)
  between operations  13.6 us (6%)
  other arithmetic  12.4 us (5%)
    all_gather x1, waiting for transfers between devices, jax.lax.all_gather(jnp.concatenate([xs, t0], axis=1), a_name, axis=0, til...  32.5 us
    reduce_scatter x1, waiting for transfers between devices, per_device(): lax.psum_scatter(jnp.dot(attended, out_weight, preferred_element_type=jnp...  32.4 us
    all_to_all x1, starting transfers between devices, per_device(): lax.all_to_all(column_layout(query_heads), 'seq', split_axis=1, concat_ax...  20.4 us
    all_to_all x1, waiting for transfers between devices, per_device(): lax.all_to_all(column_layout(query_heads), 'seq', split_axis=1, concat_ax...  16.3 us
    dynamic_slice x16, local copies, waits for them, and re-layouts, inner(): part_v = lax.dynamic_slice_in_dim(piece_v, offset, stride, 0)  15.9 us
    all_to_all x1, waiting for transfers between devices, per_device(): lax.all_to_all(column_moved, 'seq', split_axis=0, concat_axis=1, tiled=True)  15.7 us
    all_to_all x1, waiting for transfers between devices, per_device(): lax.all_to_all(column_layout(value_heads), 'seq', split_axis=1, concat_ax...  14.3 us
    all_to_all x1, waiting for transfers between devices, per_device(): lax.all_to_all(column_layout(key_heads), 'seq', split_axis=1, concat_axis...  11.7 us
  transfers between devices with their start and end apart: 6, of which 6 were waited for; matrix products, arithmetic and copies ran while one was open for 8% of the time, Pallas kernels for 0%

profile of v1, /device:TPU:1, one launch (start us, length us, event | category | flops | bytes accessed | tf_op | source)
XLA Modules:
  0.0 243.8 jit_solution(6792491259600552113)
XLA Ops:
  6.5 1.4 copy.55
  8.0 1.4 copy.56
  10.4 1.3 copy.54
  12.5 20.4 %all-to-all-start = ((bf16[1,128,4,128]{3,2,0,1:T(4,128)(2,1)}), bf16[1,128,4,128]{3,2,0,1:T(4,128)(2,1)S(1)}, u32[]{:S(2)}, u32[]{:S(2)}) async-start(bf16[1,128,4,128]{3,2,0,1:T(4,128)(2,1)} %bitcast.23), calls=%async_computation | async-start | bytes 262144 | tf_op jit(solution)/shard_map/all_to_all | solution.py:60
  33.6 1.4 fusion.48
  35.0 16.3 %all-to-all-done = bf16[1,128,4,128]{3,2,0,1:T(4,128)(2,1)S(1)} async-done(((bf16[1,128,4,128]{3,2,0,1:T(4,128)(2,1)}), bf16[1,128,4,128]{3,2,0,1:T(4,128)(2,1)S(1)}, u32[]{:S(2)}, u32[]{:S(2)}) %all-to-all-start) | async-done | bytes 131104 | tf_op jit(solution)/shard_map/all_to_all | solution.py:60
  51.3 6.3 %all-to-all-start.1 = ((bf16[1,128,4,128]{3,2,0,1:T(4,128)(2,1)}), bf16[1,128,4,128]{3,2,0,1:T(4,128)(2,1)S(1)}, u32[]{:S(2)}, u32[]{:S(2)}) async-start(bf16[1,128,4,128]{3,2,0,1:T(4,128)(2,1)} %bitcast.26), calls=%async_computation.1 | async-start | bytes 262144 | tf_op jit(solution)/shard_map/all_to_all | solution.py:63
  59.4 1.4 fusion.30
  60.8 2.9 %fusion.15 = (f32[2,512]{1,0:T(2,128)S(1)}, f32[2,512,512]{1,2,0:T(8,128)}) fusion(pred[512,512]{0,1:T(8,128)(4,1)S(1)} %iota_compare_fusion, bf16[1,512,4,128]{1,3,2,0:T(8,128)(2,1)} %bitcast.141, bf16[1,512,4,128]{1,3,2,0:T(8,128)(2,1)S(1)} %bitcast.132), kind=kOutput, calls=%fused_computation.29 | convolution fusion | flops 135789568 | bytes 2887680 | tf_op jit(solution)/shard_map/rifd,rjfd->rfij/dot_general | solution.py:88
  63.7 11.7 %all-to-all-done.1 = bf16[1,128,4,128]{3,2,0,1:T(4,128)(2,1)S(1)} async-done(((bf16[1,128,4,128]{3,2,0,1:T(4,128)(2,1)}), bf16[1,128,4,128]{3,2,0,1:T(4,128)(2,1)S(1)}, u32[]{:S(2)}, u32[]{:S(2)}) %all-to-all-start.1) | async-done | bytes 131104 | tf_op jit(solution)/shard_map/all_to_all | solution.py:63
  75.4 7.0 %all-to-all-start.2 = ((bf16[1,128,4,128]{3,2,0,1:T(4,128)(2,1)}), bf16[1,128,4,128]{3,2,0,1:T(4,128)(2,1)S(1)}, u32[]{:S(2)}, u32[]{:S(2)}) async-start(bf16[1,128,4,128]{3,2,0,1:T(4,128)(2,1)} %bitcast.29), calls=%async_computation.2 | async-start | bytes 262144 | tf_op jit(solution)/shard_map/all_to_all | solution.py:66
  83.3 2.3 fusion.23
  85.8 14.3 %all-to-all-done.2 = bf16[1,128,4,128]{3,2,0,1:T(4,128)(2,1)S(1)} async-done(((bf16[1,128,4,128]{3,2,0,1:T(4,128)(2,1)}), bf16[1,128,4,128]{3,2,0,1:T(4,128)(2,1)S(1)}, u32[]{:S(2)}, u32[]{:S(2)}) %all-to-all-start.2) | async-done | bytes 131104 | tf_op jit(solution)/shard_map/all_to_all | solution.py:66
  101.1 6.8 %all-to-all-start.3 = ((bf16[128,1,4,128]{3,2,1,0:T(4,128)(2,1)}), bf16[128,1,4,128]{3,2,1,0:T(4,128)(2,1)S(1)}, u32[]{:S(2)}, u32[]{:S(2)}) async-start(bf16[128,1,4,128]{3,2,1,0:T(4,128)(2,1)} %copy.67), calls=%async_computation.3 | async-start | bytes 262144 | tf_op jit(solution)/shard_map/all_to_all | solution.py:133
  108.2 2.2 fusion.17
  110.4 1.7 convolution_bitcast_fusion.1
  112.1 15.7 %all-to-all-done.3 = bf16[128,1,4,128]{3,2,1,0:T(4,128)(2,1)S(1)} async-done(((bf16[128,1,4,128]{3,2,1,0:T(4,128)(2,1)}), bf16[128,1,4,128]{3,2,1,0:T(4,128)(2,1)S(1)}, u32[]{:S(2)}, u32[]{:S(2)}) %all-to-all-start.3) | async-done | bytes 131104 | tf_op jit(solution)/shard_map/all_to_all | solution.py:133
  128.0 32.5 %all-gather.2.cloned.1.call-done = bf16[128,4,32,128]{3,2,1,0:T(8,128)(2,1)} async-done(((bf16[1,4,32,128]{3,2,1,0:T(8,128)(2,1)}), bf16[128,4,32,128]{3,2,1,0:T(8,128)(2,1)}) %all-gather.2.cloned.1.call-update) | async-done | bytes 4194320 | tf_op jit(solution)/shard_map/all_gather | solution.py:13
  160.4 5.2 %fusion.46 = (bf16[128,2,32,128]{3,2,1,0:T(8,128)(2,1)}, bf16[128,2,32,128]{3,2,1,0:T(8,128)(2,1)}) fusion(bf16[128,4,32,128]{3,2,1,0:T(8,128)(2,1)} %all-gather.2.cloned.1.call-done), kind=kLoop, calls=%fused_computation.79 | loop fusion | bytes 8388608 | tf_op jit(solution)/shard_map/split | solution.py:12
  165.6 36.1 %while.17 = (s32[]{:T(128)}, f32[1,2,512]{2,1,0:T(2,128)S(1)}, f32[1,2,512]{2,1,0:T(2,128)S(1)}, f32[1,2,512,128]{2,3,1,0:T(8,128)S(1)}, s32[1,2,16]{2,1,0:T(2,1...) while((s32[]{:T(128)}, f32[1,2,512]{2,1,0:T(2,128)S(1)}, ...), condition=%wide.region_10.11_spmd, body=%wide.region_6.10_spmd.sunk | while | flops 136843296 | bytes 5309099 | solution.py:129
  165.6 1.0 constant_dynamic-slice_fusion.3
  170.2 1.0 constant_dynamic-slice_fusion.3
  172.4 1.0 constant_dynamic-slice_fusion.3
  174.7 1.0 constant_dynamic-slice_fusion.3
  176.9 1.0 constant_dynamic-slice_fusion.3
  179.2 1.0 constant_dynamic-slice_fusion.3
  190.5 1.0 constant_dynamic-slice_fusion.3
  192.7 1.0 constant_dynamic-slice_fusion.3
  195.0 1.0 constant_dynamic-slice_fusion.3
  197.3 1.0 constant_dynamic-slice_fusion.3
  201.9 2.6 %convolution_convert_fusion = bf16[512,2048]{1,0:T(8,128)(2,1)} fusion(bf16[512,512]{0,1:T(8,128)(2,1)S(1)} %bitcast.142, bf16[512,2048]{1,0:T(8,128)(2,1)S(1)} %copy-done), kind=kOutput, calls=%fused_computation.26 | convolution fusion | flops 1074790400 | bytes 4718592 | tf_op jit(solution)/shard_map/dot_general | solution.py:140
  204.5 32.4 %reduce-scatter.2.cloned.1.call-done = bf16[128,2048]{1,0:T(8,128)(2,1)} async-done(((bf16[512,2048]{1,0:T(8,128)(2,1)}), bf16[128,2048]{1,0:T(8,128)(2,1)}) %reduce-scatter.2.cloned.1.call-update) | async-done | bytes 524304 | tf_op jit(solution)/shard_map/reduce_scatter | solution.py:139
  (205 shorter events, 32.0 us)
Async XLA Ops:
  6.5 195.4 %copy-start = (bf16[512,2048]{1,0:T(8,128)(2,1)S(1)}, bf16[512,2048]{1,0:T(8,128)(2,1)}, u32[]{:S(2)}) copy-start(bf16[512,2048]{1,0:T(8,128)(2,1)} %param.11) | copy-start | bytes 6291460
  6.5 153.9 %all-gather.2.cloned.1.call-start = ((), (), s32[]{:S(2)}) async-start(), calls=%async_computation.5 | async-start | bytes 4227072 | tf_op jit(solution)/shard_map/all_gather | solution.py:13
  7.9 27.0 %copy-start.3 = (bf16[512,512]{0,1:T(8,128)(2,1)}, bf16[512,512]{0,1:T(8,128)(2,1)S(1)}, u32[]{:S(2)}) copy-start(bf16[512,512]{0,1:T(8,128)(2,1)S(1)} %copy.55) | copy-start | bytes 1572868
  9.4 1.0 copy-start.2
  12.5 38.9 %all-to-all-start = ((bf16[1,128,4,128]{3,2,0,1:T(4,128)(2,1)}), bf16[1,128,4,128]{3,2,0,1:T(4,128)(2,1)S(1)}, u32[]{:S(2)}, u32[]{:S(2)}) async-start(bf16[1,128,4,128]{3,2,0,1:T(4,128)(2,1)} %bitcast.23), calls=%async_computation | async-start | bytes 262144 | tf_op jit(solution)/shard_map/all_to_all | solution.py:60
  51.3 24.1 %all-to-all-start.1 = ((bf16[1,128,4,128]{3,2,0,1:T(4,128)(2,1)}), bf16[1,128,4,128]{3,2,0,1:T(4,128)(2,1)S(1)}, u32[]{:S(2)}, u32[]{:S(2)}) async-start(bf16[1,128,4,128]{3,2,0,1:T(4,128)(2,1)} %bitcast.26), calls=%async_computation.1 | async-start | bytes 262144 | tf_op jit(solution)/shard_map/all_to_all | solution.py:63
  75.4 24.7 %all-to-all-start.2 = ((bf16[1,128,4,128]{3,2,0,1:T(4,128)(2,1)}), bf16[1,128,4,128]{3,2,0,1:T(4,128)(2,1)S(1)}, u32[]{:S(2)}, u32[]{:S(2)}) async-start(bf16[1,128,4,128]{3,2,0,1:T(4,128)(2,1)} %bitcast.29), calls=%async_computation.2 | async-start | bytes 262144 | tf_op jit(solution)/shard_map/all_to_all | solution.py:66
  83.3 2.3 copy-start.6
  101.1 26.7 %all-to-all-start.3 = ((bf16[128,1,4,128]{3,2,1,0:T(4,128)(2,1)}), bf16[128,1,4,128]{3,2,1,0:T(4,128)(2,1)S(1)}, u32[]{:S(2)}, u32[]{:S(2)}) async-start(bf16[128,1,4,128]{3,2,1,0:T(4,128)(2,1)} %copy.67), calls=%async_computation.3 | async-start | bytes 262144 | tf_op jit(solution)/shard_map/all_to_all | solution.py:133
  107.9 129.1 %reduce-scatter.2.cloned.1.call-start = ((), (), s32[]{:S(2)}) async-start(), calls=%async_computation.6 | async-start | bytes 2621440 | tf_op jit(solution)/shard_map/reduce_scatter | solution.py:139
  108.2 2.2 copy-start.1
  127.9 37.7 %copy-start.5 = (s32[1,2,16]{2,1,0:T(2,128)S(1)}, s32[1,2,16]{2,1,0:T(2,128)}, u32[]{:S(2)}) copy-start(s32[1,2,16]{2,1,0:T(2,128)} %param.10) | copy-start | bytes 388
  165.6 36.2 %copy-start.4 = (bf16[1,512,1,128]{1,3,2,0:T(8,128)(2,1)S(1)}, bf16[1,512,1,128]{1,3,2,0:T(8,128)(2,1)}, u32[]{:S(2)}) copy-start(bf16[1,512,1,128]{1,3,2,0:T(8,128)(2,1)} %fusion.23) | copy-start | bytes 393220
Sparse Core Ops, SparseCore 0:
  10.6 149.8 all-gather.1
  204.7 32.2 reduce-scatter.1
